TPU v7x, 32 devices: a whole 2x2x4 slice. The times are simulated.
32 devices in a mesh: groups: 2 (over x), seq: 4 (over z), expert: 4 (over y, core).
Axes of the slice: x: 2, y: 2, z: 4, core: 2. Of those that a mesh axis runs over, the one named last changes fastest.
Arguments:
- q_lat: bfloat16 [512, 65536], P(('groups', 'seq'), 'expert'), parts along dimension 0, may hold values from -36 to 36
- q_rope: bfloat16 [512, 8192], P(('groups', 'seq'), 'expert'), parts along dimension 0, may hold values from -6 to 6
- cache_lat: bfloat16 [2048, 512], P(('groups', 'seq')), parts along dimension 0, may hold values from -7 to 7
- cache_rope: bfloat16 [2048, 64], P(('groups', 'seq')), parts along dimension 0, may hold values from -8 to 8
- tool_lat: bfloat16 [256, 512], P(('groups', 'seq')), parts along dimension 0, may hold values from -2.5 to 2.5
- tool_rope: bfloat16 [256, 64], P(('groups', 'seq')), parts along dimension 0, may hold values from -8 to 8
- offset: int32 [2], P('groups'), parts along dimension 0, may hold values from 512 to 736
- suf_lat: bfloat16 [512, 512], P(('groups', 'seq')), parts along dimension 0, may hold values from -6 to 6
- suf_rope: bfloat16 [512, 64], P(('groups', 'seq')), parts along dimension 0, may hold values from -8 to 8
- w_uv: bfloat16 [128, 512, 128], P('expert'), may hold values from -1 to 1
- w_out: bfloat16 [16384, 7168], P('expert', 'seq'), may hold values from -0.19921875 to 0.19921875
- resid: bfloat16 [512, 7168], P(('groups', 'expert'), 'seq'), parts along dimension 0, may hold values from -36 to 36
- routes: int32 [512, 2], P(('groups', 'expert')), parts along dimension 0, may hold values from 0 to 3, all different within a row; in each aligned block of 64 rows (0 to 63, 64 to 127, ...) at most 40 rows name the same one
- probs: float32 [512, 2], P(('groups', 'expert')), parts along dimension 0, may hold values from 0.1 to 1
- w_gate: bfloat16 [4, 7168, 1024], P('expert', None, 'seq'), may hold values from -0.0625 to 0.0625
- w_up: bfloat16 [4, 7168, 1024], P('expert', None, 'seq'), may hold values from -0.0625 to 0.0625
- w_down: bfloat16 [4, 1024, 7168], P('expert', 'seq'), may hold values from -0.1875 to 0.1875
Outputs:
- attn_residual: bfloat16 [512, 7168], P(('groups', 'expert'), 'seq'), parts along dimension 0
- expert_mix: bfloat16 [512, 7168], P(('groups', 'expert'), 'seq'), parts along dimension 0
There are 2 independent parts, one for each index of `groups`. A program takes and returns all parts, laid end to end along the dimension named above; an argument that names none is the same for every part. Nothing has to cross between parts.
Inputs may be any that keep to these rules, and one draw needn't show every extreme that they name: `routes`: within the rows of one device of the expert axis (64 rows in a row), no expert is named more than 40 times.
All inputs are finite; a program needn't handle non-finite values.
Results may differ from a plain program's by a relative error of at most 0.03.
Values may be sent and summed in bfloat16 or wider, within the bound.
No kernel may reach another device: no remote copies, remote signals or barrier semaphores. Data moves between devices by JAX's collectives and lax.ppermute only.
A program may use at most 128 MiB of HBM per device.

v0:
```python
import jax
import jax.numpy as jnp
from jax import lax
from jax.sharding import PartitionSpec as P

score_scale = 192.0 ** (-0.5)
floor_score = -1e30
norm_eps = 1e-06


def run_expert(tokens_in, w_gate, w_up, w_down):
    sources, count, width = tokens_in.shape
    rows = tokens_in.reshape(sources * count, width)
    gate = jnp.dot(rows, w_gate[0], preferred_element_type=jnp.float32)
    upper = jnp.dot(rows, w_up[0], preferred_element_type=jnp.float32)
    inner = (jax.nn.silu(gate) * upper).astype(jnp.bfloat16)
    partial_out = jnp.dot(inner, w_down[0], preferred_element_type=jnp.float32).reshape(
        sources, count, width
    )
    summed = lax.psum_scatter(
        partial_out.astype(jnp.bfloat16), "seq", scatter_dimension=2, tiled=True
    )
    return lax.all_to_all(summed, "expert", split_axis=0, concat_axis=0, tiled=True)


def on_device(
    q_lat,
    q_rope,
    cache_lat,
    cache_rope,
    tool_lat,
    tool_rope,
    offset,
    suf_lat,
    suf_rope,
    w_uv,
    w_out,
    resid,
    routes,
    probs,
    w_gate,
    w_up,
    w_down,
):
    seq_index = lax.axis_index("seq")
    ctx_dev = cache_lat.shape[0]
    query_dev = q_lat.shape[0]
    heads_dev, lat_width, value_width = w_uv.shape
    rope_width = cache_rope.shape[1]
    tool_all_lat, tool_all_rope = (
        lax.all_gather(tool_lat, "seq", axis=0, tiled=True),
        lax.all_gather(tool_rope, "seq", axis=0, tiled=True),
    )
    tool_len = tool_all_lat.shape[0]
    position = seq_index * ctx_dev + jnp.arange(ctx_dev, dtype=jnp.int32)
    shifted = position - offset[0]
    inside = (shifted >= 0) & (shifted < tool_len)
    safe = jnp.clip(shifted, 0, tool_len - 1)
    ctx_lat = jnp.where(inside[:, None], jnp.take(tool_all_lat, safe, axis=0), cache_lat)
    ctx_rope = jnp.where(inside[:, None], jnp.take(tool_all_rope, safe, axis=0), cache_rope)
    local_lat = jnp.concatenate([ctx_lat, suf_lat], axis=0)
    local_rope = jnp.concatenate([ctx_rope, suf_rope], axis=0)
    block_len = ctx_dev + query_dev
    query_rows = query_dev * heads_dev
    queries_lat = q_lat.reshape(query_rows, lat_width)
    queries_rope = q_rope.reshape(query_rows, rope_width)
    query_pos = seq_index * query_dev + jnp.arange(query_rows, dtype=jnp.int32) // heads_dev
    running_max = jnp.full((query_rows,), floor_score, jnp.float32)
    piece_lat = lax.all_gather(local_lat, "seq", axis=0, tiled=True)
    piece_rope = lax.all_gather(local_rope, "seq", axis=0, tiled=True)
    global_row = jnp.arange(piece_lat.shape[0], dtype=jnp.int32)
    within = global_row % block_len
    owner = global_row // block_len
    is_context = within < ctx_dev
    suffix_pos = owner * query_dev + within - ctx_dev
    visible = is_context[None, :] | (suffix_pos[None, :] <= query_pos[:, None])
    scores = jnp.einsum("qc,kc->qk", queries_lat, piece_lat, preferred_element_type=jnp.float32)
    scores = (
        scores
        + jnp.einsum("qc,kc->qk", queries_rope, piece_rope, preferred_element_type=jnp.float32)
    ) * score_scale
    scores = jnp.where(visible, scores, floor_score)
    new_max = jnp.maximum(running_max, jnp.max(scores, axis=1))
    weights = jnp.where(visible, jnp.exp(scores - new_max[:, None]), 0.0)
    new_total = jnp.sum(weights, axis=1)
    new_acc = jnp.dot(weights.astype(jnp.bfloat16), piece_lat, preferred_element_type=jnp.float32)
    latent_out = (
        (new_acc / new_total[:, None]).astype(jnp.bfloat16).reshape(query_dev, heads_dev, lat_width)
    )
    head_vals = jnp.einsum(
        "thc,hcv->thv", latent_out, w_uv, preferred_element_type=jnp.float32
    ).astype(jnp.bfloat16)
    head_vals = head_vals.reshape(query_dev, heads_dev * value_width)
    all_values = lax.all_gather(head_vals, "seq", axis=0, tiled=True)
    tok_dev = resid.shape[0]
    attn_sum = lax.psum_scatter(
        jnp.dot(all_values, w_out, preferred_element_type=jnp.float32).astype(jnp.bfloat16),
        "expert",
        scatter_dimension=0,
        tiled=True,
    ).astype(jnp.float32)
    attn_residual = (resid.astype(jnp.float32) + attn_sum).astype(jnp.bfloat16)
    expert_count = lax.axis_size("expert") * w_gate.shape[0]
    top_count = routes.shape[1]
    capacity = tok_dev * top_count * 5 // (4 * expert_count)
    flat_routes = routes.reshape(-1)
    one_hot = (flat_routes[:, None] == jnp.arange(expert_count, dtype=jnp.int32)[None, :]).astype(
        jnp.int32
    )
    earlier = jnp.cumsum(one_hot, axis=0) - one_hot
    slot = jnp.sum(earlier * one_hot, axis=1)
    target = (flat_routes * capacity + slot).reshape(tok_dev, top_count)
    slot_ids = jnp.arange(expert_count * capacity, dtype=jnp.int32)
    matches = slot_ids[:, None, None] == target[None, :, :]
    send_matrix = jnp.any(matches, axis=2).astype(jnp.bfloat16)
    route_weight = 2.5 * probs / jnp.sum(probs, axis=1, keepdims=True)
    gather_matrix = jnp.sum(jnp.where(matches, route_weight[None, :, :], 0.0), axis=2).T
    whole_stream = lax.all_gather(attn_residual, "seq", axis=1, tiled=True).astype(jnp.float32)
    normed = (
        whole_stream
        * lax.rsqrt(jnp.mean(whole_stream * whole_stream, axis=1, keepdims=True) + norm_eps)
    ).astype(jnp.bfloat16)
    outgoing = jnp.dot(send_matrix, normed, preferred_element_type=jnp.float32).astype(jnp.bfloat16)
    outgoing = outgoing.reshape(expert_count, capacity, normed.shape[1])
    returned = run_expert(
        lax.all_to_all(outgoing, "expert", split_axis=0, concat_axis=0, tiled=True),
        w_gate,
        w_up,
        w_down,
    )
    returned = returned.reshape(expert_count * capacity, returned.shape[2]).astype(jnp.float32)
    expert_mix = jnp.dot(
        gather_matrix, returned, precision=lax.Precision.HIGHEST, preferred_element_type=jnp.float32
    )
    return (attn_residual, expert_mix.astype(jnp.bfloat16))


def solution(mesh):
    placed = (
        P(("groups", "seq"), "expert"),
        P(("groups", "seq"), "expert"),
        P(("groups", "seq"), None),
        P(("groups", "seq"), None),
        P(("groups", "seq"), None),
        P(("groups", "seq"), None),
        P("groups"),
        P(("groups", "seq"), None),
        P(("groups", "seq"), None),
        P("expert", None, None),
        P("expert", "seq"),
        P(("groups", "expert"), "seq"),
        P(("groups", "expert"), None),
        P(("groups", "expert"), None),
        P("expert", None, "seq"),
        P("expert", None, "seq"),
        P("expert", "seq", None),
    )
    return jax.shard_map(
        on_device,
        mesh=mesh,
        in_specs=placed,
        out_specs=(P(("groups", "expert"), "seq"), P(("groups", "expert"), "seq")),
        check_vma=False,
    )
```

profile of v0, /device:TPU:0, one launch (start us, length us, event | category | flops | bytes accessed | tf_op | source)
XLA Modules:
  0.0 289.8 jit_solution(17597389861939251030)
XLA Ops:
  8.1 15.3 %all_gather.18 = bf16[128,512]{1,0:T(8,128)(2,1)S(1)} all-gather(bf16[32,512]{1,0:T(8,128)(2,1)} %param.21), channel_id=1, replica_groups=mesh['groups'=2,'seq'=4,'expert'=4] {'seq'}, dimensions={0}, use_global_device_ids=true | all-gather | bytes 163840 | tf_op jit(solution)/shard_map/all_gather | solution.py:51
  23.4 1.2 gather_fusion
  24.5 1.1 select_select_fusion
  25.7 1.6 pad_maximum_fusion
  27.4 2.4 reshape.119
  29.7 13.2 %all_gather.20 = bf16[128,64]{1,0:T(8,128)(2,1)S(1)} all-gather(bf16[32,64]{1,0:T(8,128)(2,1)S(1)} %copy-done.8), channel_id=1, replica_groups=mesh['groups'=2,'seq'=4,'expert'=4] {'seq'}, dimensions={0}, use_global_device_ids=true | all-gather | bytes 20480 | tf_op jit(solution)/shard_map/all_gather | solution.py:52
  43.0 0.9 gather_fusion.1
  44.3 15.6 %all-gather = bf16[4,320,64]{1,2,0:T(8,128)(2,1)S(1)} all-gather(bf16[1,320,64]{1,2,0:T(8,128)(2,1)S(1)} %copy.59), channel_id=1, replica_groups=mesh['groups'=2,'seq'=4,'expert'=4] {'seq'}, dimensions={0}, use_global_device_ids=true | all-gather | bytes 204800 | tf_op jit(solution)/shard_map/all_gather | solution.py:70
  60.2 0.5 reshape.120
  60.8 3.9 %all-gather.4.cloned.1.call-done = bf16[1280,512]{1,0:T(8,128)(2,1)} async-done(((bf16[320,512]{1,0:T(8,128)(2,1)}), bf16[1280,512]{1,0:T(8,128)(2,1)}) %all-gather.4.cloned.1.call-update) | async-done | bytes 1310736 | tf_op jit(solution)/shard_map/all_gather | solution.py:69
  64.7 5.0 %fusion.51 = f32[1280,2048]{1,0:T(8,128)S(1)} fusion(bf16[1280,512]{1,0:T(8,128)(2,1)} %all-gather.4.cloned.1.call-done, bf16[2048,512]{1,0:T(8,128)(2,1)} %reshape.119), kind=kOutput, calls=%fused_computation.80 | convolution fusion | flops 2684354560 | bytes 13893632 | tf_op jit(solution)/shard_map/qc,kc->qk/dot_general | solution.py:77
  69.6 4.1 %fusion.50 = (f32[2048]{0:T(1024)S(1)}, f32[2048,1280]{0,1:T(8,128)S(1)}) fusion(f32[1280,2048]{1,0:T(8,128)S(1)} %fusion.51, bf16[1280,64]{0,1:T(8,128)(2,1)S(1)} %reshape.143, bf16[2048,64]{1,0:T(8,128)(2,1)S(1)} %reshape.120, s32[2048]{0:T(1024)S(1)} %fusion.40, s32[1280]{0:T(1024)S(1)} %fusion.38, pred[1280]{0:T(1024)(128)(4,1)S(1)} %fusion.45), kind=kOutput, calls=%fused_computation.79 | convolution fusion | flops 351270912 | bytes 21420288 | tf_op jit(solution)/shard_map/qc,kc->qk/dot_general | solution.py:80
  73.7 3.9 %fusion = f32[2048]{0:T(1024)S(1)} fusion(f32[2048,1280]{0,1:T(8,128)S(1)} %get-tuple-element.3, f32[2048]{0:T(1024)S(1)} %broadcast_maximum_fusion, s32[2048]{0:T(1024)S(1)} %fusion.40, s32[1280]{0:T(1024)S(1)} %fusion.38, pred[1280]{0:T(1024)(128)(4,1)S(1)} %fusion.45), kind=kLoop, calls=%fused_computation.7 | loop fusion | flops 13105152 | bytes 10516736 | tf_op jit(solution)/shard_map/reduce_sum | solution.py:85
  77.7 4.5 %divide_convert_fusion = bf16[2048,512]{1,0:T(8,128)(2,1)S(1)} fusion(f32[2048]{0:T(1024)S(1)} %fusion, bf16[1280,512]{1,0:T(8,128)(2,1)S(1)} %copy-done.13, f32[2048,1280]{0,1:T(8,128)S(1)} %get-tuple-element.3, f32[2048]{0:T(1024)S(1)} %broadcast_maximum_fusion, s32[2048]{0:T(1024)S(1)} %fusion.40, s32[1280]{0:T(1024)S(1)} %fusion.38, ...), kind=kOutput, calls=%fused_computation.15 | convolution fusion | flops 2699558912 | bytes 13924608 | tf_op jit(solution)/shard_map/dot_general | solution.py:86
  82.3 2.5 fusion.23
  84.8 0.9 copy.73
  85.8 44.8 %all-gather.6.cloned.1.call-done = bf16[256,4096]{1,0:T(8,128)(2,1)} async-done(((bf16[64,4096]{1,0:T(8,128)(2,1)}), bf16[256,4096]{1,0:T(8,128)(2,1)}) %all-gather.6.cloned.1.call-update) | async-done | bytes 2097168 | tf_op jit(solution)/shard_map/all_gather | solution.py:94
  130.6 10.7 %convolution_convert_fusion.2 = bf16[256,1792]{1,0:T(8,128)(2,1)} fusion(bf16[256,4096]{1,0:T(8,128)(2,1)} %all-gather.6.cloned.1.call-done, bf16[4096,1792]{1,0:T(8,128)(2,1)} %param.27), kind=kOutput, calls=%fused_computation.21 | convolution fusion | flops 3758555136 | bytes 17694720 | tf_op jit(solution)/shard_map/dot_general | solution.py:97
  142.7 21.6 %reduce-scatter.3.cloned.1.call-done = bf16[64,1792]{1,0:T(8,128)(2,1)} async-done(((bf16[256,1792]{1,0:T(8,128)(2,1)}), bf16[64,1792]{1,0:T(8,128)(2,1)}) %reduce-scatter.3.cloned.1.call-update) | async-done | bytes 229392 | tf_op jit(solution)/shard_map/reduce_scatter | solution.py:96
  164.3 1.0 add_convert_fusion
  165.3 21.0 %all_gather.23 = bf16[64,7168]{1,0:T(8,128)(2,1)S(1)} all-gather(bf16[64,1792]{1,0:T(8,128)(2,1)S(1)} %add_convert_fusion), channel_id=1, replica_groups=mesh['groups'=2,'seq'=4,'expert'=4] {'seq'}, dimensions={1}, use_global_device_ids=true | all-gather | bytes 1146880 | tf_op jit(solution)/shard_map/all_gather | solution.py:118
  186.6 0.8 convolution_convert_fusion.1
  187.5 30.4 %all_to_all.10 = bf16[4,40,7168]{2,1,0:T(8,128)(2,1)S(1)} all-to-all(bf16[4,40,7168]{2,1,0:T(8,128)(2,1)S(1)} %bitcast.51), channel_id=1, replica_groups=mesh['groups'=2,'seq'=4,'expert'=4] {'expert'}, dimensions={0} | all-to-all | bytes 4587520 | tf_op jit(solution)/shard_map/all_to_all | solution.py:126
  217.8 0.8 fusion.12
  218.6 1.3 copy-done.11
  219.9 0.8 fusion.29
  220.7 1.3 copy-done.12
  221.9 2.2 convolution_convert_fusion
  224.1 45.3 %reduce-scatter.5.cloned.1.call-done = bf16[4,40,1792]{2,1,0:T(8,128)(2,1)} async-done(((bf16[4,40,7168]{2,1,0:T(8,128)(2,1)}), bf16[4,40,1792]{2,1,0:T(8,128)(2,1)}) %reduce-scatter.5.cloned.1.call-update) | async-done | bytes 573456 | tf_op jit(solution)/shard_map/reduce_scatter | solution.py:20
  269.4 3.5 %all-to-all-start.1 = ((bf16[4,40,1792]{2,1,0:T(8,128)(2,1)}), bf16[4,40,1792]{2,1,0:T(8,128)(2,1)S(1)}, u32[]{:S(2)}, u32[]{:S(2)}) async-start(bf16[4,40,1792]{2,1,0:T(8,128)(2,1)} %reduce-scatter.5.cloned.1.call-done), calls=%async_computation.3 | async-start | bytes 1146880 | tf_op jit(solution)/shard_map/all_to_all | solution.py:23
  273.1 9.2 %all-to-all-done.1 = bf16[4,40,1792]{2,1,0:T(8,128)(2,1)S(1)} async-done(((bf16[4,40,1792]{2,1,0:T(8,128)(2,1)}), bf16[4,40,1792]{2,1,0:T(8,128)(2,1)S(1)}, u32[]{:S(2)}, u32[]{:S(2)}) %all-to-all-start.1) | async-done | bytes 573472 | tf_op jit(solution)/shard_map/all_to_all | solution.py:23
  282.2 1.1 convolution_convert_fusion.3
  (61 shorter events, 2.7 us)
Async XLA Ops:
  7.2 20.2 %copy-start.2 = (bf16[64,16384]{1,0:T(8,128)(2,1)S(1)}, bf16[64,16384]{1,0:T(8,128)(2,1)}, u32[]{:S(2)}) copy-start(bf16[64,16384]{1,0:T(8,128)(2,1)} %param.17) | copy-start | bytes 6291460
  7.2 57.5 %all-gather.4.cloned.1.call-start = ((), (), s32[]{:S(2)}) async-start(), calls=%async_computation.4 | async-start | bytes 1638400 | tf_op jit(solution)/shard_map/all_gather | solution.py:69
  23.4 6.4 %copy-start.8 = (bf16[32,64]{1,0:T(8,128)(2,1)S(1)}, bf16[32,64]{1,0:T(8,128)(2,1)}, u32[]{:S(2)}) copy-start(bf16[32,64]{1,0:T(8,128)(2,1)} %param.22) | copy-start | bytes 12292
  24.5 19.3 %copy-start.6 = (bf16[256,64]{0,1:T(8,128)(2,1)S(1)}, bf16[256,64]{0,1:T(8,128)(2,1)}, u32[]{:S(2)}) copy-start(bf16[256,64]{0,1:T(8,128)(2,1)} %param.20) | copy-start | bytes 98308
  24.5 19.6 %copy-start.7 = (bf16[64,64]{1,0:T(8,128)(2,1)S(1)}, bf16[64,64]{1,0:T(8,128)(2,1)}, u32[]{:S(2)}) copy-start(bf16[64,64]{1,0:T(8,128)(2,1)} %param.25) | copy-start | bytes 24580
  25.6 34.5 %copy-start.4 = (bf16[64,2048]{1,0:T(8,128)(2,1)S(1)}, bf16[64,2048]{1,0:T(8,128)(2,1)}, u32[]{:S(2)}) copy-start(bf16[64,2048]{1,0:T(8,128)(2,1)} %param.18) | copy-start | bytes 786436
  27.3 103.3 %all-gather.6.cloned.1.call-start = ((), (), s32[]{:S(2)}) async-start(), calls=%async_computation.5 | async-start | bytes 2621440 | tf_op jit(solution)/shard_map/all_gather | solution.py:94
  73.7 4.0 %copy-start.13 = (bf16[1280,512]{1,0:T(8,128)(2,1)S(1)}, bf16[1280,512]{1,0:T(8,128)(2,1)}, u32[]{:S(2)}) copy-start(bf16[1280,512]{1,0:T(8,128)(2,1)} %all-gather.4.cloned.1.call-done) | copy-start | bytes 3932164
  77.7 4.6 %copy-start = (bf16[32,512,128]{2,1,0:T(8,128)(2,1)S(1)}, bf16[32,512,128]{2,1,0:T(8,128)(2,1)}, u32[]{:S(2)}) copy-start(bf16[32,512,128]{2,1,0:T(8,128)(2,1)} %param.26) | copy-start | bytes 12582916
  85.7 55.9 %copy-start.9 = (s32[64,2]{0,1:T(2,128)S(1)}, s32[64,2]{0,1:T(2,128)}, u32[]{:S(2)}) copy-start(s32[64,2]{0,1:T(2,128)} %param.29) | copy-start | bytes 1540
  85.7 78.6 %copy-start.5 = (bf16[64,1792]{1,0:T(8,128)(2,1)S(1)}, bf16[64,1792]{1,0:T(8,128)(2,1)}, u32[]{:S(2)}) copy-start(bf16[64,1792]{1,0:T(8,128)(2,1)} %param.28) | copy-start | bytes 688132
  85.7 78.6 %reduce-scatter.3.cloned.1.call-start = ((), (), s32[]{:S(2)}) async-start(), calls=%async_computation.6 | async-start | bytes 1146880 | tf_op jit(solution)/shard_map/reduce_scatter | solution.py:96
  141.4 128.1 %reduce-scatter.5.cloned.1.call-start = ((), (), s32[]{:S(2)}) async-start(), calls=%async_computation.7 | async-start | bytes 2867200 | tf_op jit(solution)/shard_map/reduce_scatter | solution.py:20
  165.3 52.5 %copy-start.3 = (bf16[64,1792]{1,0:T(8,128)(2,1)}, bf16[64,1792]{1,0:T(8,128)(2,1)S(1)}, u32[]{:S(2)}) copy-start(bf16[64,1792]{1,0:T(8,128)(2,1)S(1)} %add_convert_fusion) | copy-start | bytes 688132
  186.6 31.2 %copy-start.1 = (bf16[1,7168,256]{2,1,0:T(8,128)(2,1)S(1)}, bf16[1,7168,256]{2,1,0:T(8,128)(2,1)}, u32[]{:S(2)}) copy-start(bf16[1,7168,256]{2,1,0:T(8,128)(2,1)} %param.31) | copy-start | bytes 11010052
  217.8 2.0 copy-start.11
  219.9 2.0 copy-start.12
  221.9 51.0 %copy-start.10 = (f32[64,2]{0,1:T(2,128)S(1)}, f32[64,2]{0,1:T(2,128)}, u32[]{:S(2)}) copy-start(f32[64,2]{0,1:T(2,128)} %param.30) | copy-start | bytes 1540
  269.4 12.8 %all-to-all-start.1 = ((bf16[4,40,1792]{2,1,0:T(8,128)(2,1)}), bf16[4,40,1792]{2,1,0:T(8,128)(2,1)S(1)}, u32[]{:S(2)}, u32[]{:S(2)}) async-start(bf16[4,40,1792]{2,1,0:T(8,128)(2,1)} %reduce-scatter.5.cloned.1.call-done), calls=%async_computation.3 | async-start | bytes 1146880 | tf_op jit(solution)/shard_map/all_to_all | solution.py:23
Sparse Core Ops, SparseCore 0:
  27.4 37.1 all-gather.3
  85.8 44.7 all-gather.5
  141.5 22.7 reduce-scatter.2
  224.3 45.1 reduce-scatter.4
where the time goes:
time: 290 us
  waiting for transfers between devices  125 us (43%)
  blocking collectives  95.5 us (33%)
  matrix products  32.4 us (11%)
  between operations  14.9 us (5%)
  local copies, waits for them, and re-layouts  9.37 us (3%)
  other arithmetic  8.86 us (3%)
  starting transfers between devices  3.86 us (1%)
    reduce_scatter x1, waiting for transfers between devices, run_expert(): lax.psum_scatter(partial_out.astype(jnp.bfloat16), 'seq', scatter_dimensi...  45.3 us
    all_gather x1, waiting for transfers between devices, on_device(): all_values = lax.all_gather(head_vals, 'seq', axis=0, tiled=True)  44.8 us
    all_to_all x1, blocking collectives, on_device(): lax.all_to_all(outgoing, 'expert', split_axis=0, concat_axis=0, tiled=True)  30.4 us
    reduce_scatter x1, waiting for transfers between devices, on_device(): lax.psum_scatter(jnp.dot(all_values, w_out, preferred_element_type=jnp.fl...  21.6 us
    all_gather x1, blocking collectives, on_device(): lax.all_gather(attn_residual, 'seq', axis=1, tiled=True).astype(jnp.float32)  21 us
    all_gather x1, blocking collectives, on_device(): piece_rope = lax.all_gather(local_rope, 'seq', axis=0, tiled=True)  15.6 us
    all_gather x1, blocking collectives, on_device(): lax.all_gather(tool_lat, 'seq', axis=0, tiled=True)  15.3 us
    all_gather x1, blocking collectives, on_device(): lax.all_gather(tool_rope, 'seq', axis=0, tiled=True)  13.2 us
  transfers between devices with their start and end apart: 5, of which 5 were waited for; matrix products, arithmetic and copies ran while one was open for 2% of the time, Pallas kernels for 0%

commit v1 on v0

--- a/solution.py
+++ b/solution.py
@@ -66,8 +66,13 @@
     queries_rope = q_rope.reshape(query_rows, rope_width)
     query_pos = seq_index * query_dev + jnp.arange(query_rows, dtype=jnp.int32) // heads_dev
     running_max = jnp.full((query_rows,), floor_score, jnp.float32)
-    piece_lat = lax.all_gather(local_lat, "seq", axis=0, tiled=True)
-    piece_rope = lax.all_gather(local_rope, "seq", axis=0, tiled=True)
+    piece_lat, piece_rope = jnp.split(
+        lax.all_gather(
+            jnp.concatenate([local_lat, local_rope], axis=1), axis_name="seq", axis=0, tiled=True
+        ),
+        [local_lat.shape[1]],
+        axis=1,
+    )
     global_row = jnp.arange(piece_lat.shape[0], dtype=jnp.int32)
     within = global_row % block_len
     owner = global_row // block_len

time: 290 us -> 306 us (1.055)
  waiting for transfers between devices: 125 us -> 158 us
  blocking collectives: 95.5 us -> 80.2 us
    all_gather x1, waiting for transfers between devices: 3.91 us -> 36.6 us  [on_device(): lax.all_gather(jnp.concatenate([local_lat, local_rope], axis=1), axis_nam...]
    all_gather x1 -> x0, blocking collectives: 15.6 us -> none  [on_device(): piece_rope = lax.all_gather(local_rope, 'seq', axis=0, tiled=True)]
  transfers between devices with their start and end apart: 5 -> 5, of which waited for: 5 -> 5; matrix products, arithmetic and copies ran while one was open for 2% -> 1% of each run, Pallas kernels for 0% -> 0%
where the time goes in v1:
time: 306 us
  waiting for transfers between devices  158 us (52%)
  blocking collectives  80.2 us (26%)
  matrix products  31.6 us (10%)
  between operations  14.9 us (5%)
  local copies, waits for them, and re-layouts  9.72 us (3%)
  other arithmetic  7.99 us (3%)
  starting transfers between devices  3.64 us (1%)
    reduce_scatter x1, waiting for transfers between devices, run_expert(): lax.psum_scatter(partial_out.astype(jnp.bfloat16), 'seq', scatter_dimensi...  45.3 us
    all_gather x1, waiting for transfers between devices, on_device(): all_values = lax.all_gather(head_vals, 'seq', axis=0, tiled=True)  44.6 us
    all_gather x1, waiting for transfers between devices, on_device(): lax.all_gather(jnp.concatenate([local_lat, local_rope], axis=1), axis_nam...  36.6 us
    all_to_all x1, blocking collectives, on_device(): lax.all_to_all(outgoing, 'expert', split_axis=0, concat_axis=0, tiled=True)  30.6 us
    reduce_scatter x1, waiting for transfers between devices, on_device(): lax.psum_scatter(jnp.dot(all_values, w_out, preferred_element_type=jnp.fl...  21.9 us
    all_gather x1, blocking collectives, on_device(): lax.all_gather(attn_residual, 'seq', axis=1, tiled=True).astype(jnp.float32)  21 us
    all_gather x1, blocking collectives, on_device(): lax.all_gather(tool_lat, 'seq', axis=0, tiled=True)  15.3 us
    all_gather x1, blocking collectives, on_device(): lax.all_gather(tool_rope, 'seq', axis=0, tiled=True)  13.3 us
  transfers between devices with their start and end apart: 5, of which 5 were waited for; matrix products, arithmetic and copies ran while one was open for 1% of the time, Pallas kernels for 0%

profile of v1, /device:TPU:0, one launch (start us, length us, event | category | flops | bytes accessed | tf_op | source)
XLA Modules:
  0.0 305.7 jit_solution(8582636202565000320)
XLA Ops:
  8.1 15.3 %all_gather.15 = bf16[128,512]{1,0:T(8,128)(2,1)S(1)} all-gather(bf16[32,512]{1,0:T(8,128)(2,1)} %param.21), channel_id=1, replica_groups=mesh['groups'=2,'seq'=4,'expert'=4] {'seq'}, dimensions={0}, use_global_device_ids=true | all-gather | bytes 163840 | tf_op jit(solution)/shard_map/all_gather | solution.py:51
  23.4 13.3 %all_gather.16 = bf16[128,64]{1,0:T(8,128)(2,1)S(1)} all-gather(bf16[32,64]{1,0:T(8,128)(2,1)} %param.22), channel_id=1, replica_groups=mesh['groups'=2,'seq'=4,'expert'=4] {'seq'}, dimensions={0}, use_global_device_ids=true | all-gather | bytes 20480 | tf_op jit(solution)/shard_map/all_gather | solution.py:52
  36.7 1.2 gather_fusion
  37.9 0.9 gather_fusion.1
  38.7 0.9 copy.39
  39.6 1.1 select_select_fusion
  40.9 0.8 maximum_maximum_fusion
  41.8 2.4 reshape.119
  44.1 0.5 reshape.120
  44.7 36.6 %all-gather.3.cloned.1.call-done = bf16[1280,576]{1,0:T(8,128)(2,1)} async-done(((bf16[320,576]{1,0:T(8,128)(2,1)}), bf16[1280,576]{1,0:T(8,128)(2,1)}) %all-gather.3.cloned.1.call-update) | async-done | bytes 1474576 | tf_op jit(solution)/shard_map/all_gather | solution.py:70
  81.3 5.1 %fusion.27 = f32[1280,2048]{1,0:T(8,128)S(1)} fusion(bf16[2048,512]{1,0:T(8,128)(2,1)} %reshape.119, bf16[1280,576]{1,0:T(8,128)(2,1)} %all-gather.3.cloned.1.call-done), kind=kOutput, calls=%fused_computation.32 | convolution fusion | flops 2684354560 | bytes 13893632 | tf_op jit(solution)/shard_map/qc,kc->qk/dot_general | solution.py:82
  86.4 3.2 %fusion.54 = (f32[2048]{0:T(1024)S(1)}, f32[2048,1280]{0,1:T(8,128)S(1)}) fusion(f32[1280,2048]{1,0:T(8,128)S(1)} %fusion.27, bf16[2048,64]{1,0:T(8,128)(2,1)S(1)} %reshape.120, bf16[1280,576]{1,0:T(8,128)(2,1)S(1)} %copy-done.7, s32[2048]{0:T(1024)S(1)} %fusion.44, s32[1280]{0:T(1024)S(1)} %fusion.42, pred[1280]{0:T(1024)(128)(4,1)S(1)} %fusion.49), kind=kOutput, calls=%fused_computation.82 | convolution fusion | flops 351270912 | bytes 21850112 | tf_op jit(solution)/shard_map/qc,kc->qk/dot_general | solution.py:85
  89.6 3.9 %fusion = f32[2048]{0:T(1024)S(1)} fusion(f32[2048,1280]{0,1:T(8,128)S(1)} %get-tuple-element.3, f32[2048]{0:T(1024)S(1)} %broadcast_maximum_fusion, s32[2048]{0:T(1024)S(1)} %fusion.44, s32[1280]{0:T(1024)S(1)} %fusion.42, pred[1280]{0:T(1024)(128)(4,1)S(1)} %fusion.49), kind=kLoop, calls=%fused_computation.7 | loop fusion | flops 13105152 | bytes 10516736 | tf_op jit(solution)/shard_map/reduce_sum | solution.py:90
  93.6 4.5 %divide_convert_fusion = bf16[2048,512]{1,0:T(8,128)(2,1)S(1)} fusion(f32[2048]{0:T(1024)S(1)} %fusion, f32[2048,1280]{0,1:T(8,128)S(1)} %get-tuple-element.3, f32[2048]{0:T(1024)S(1)} %broadcast_maximum_fusion, s32[2048]{0:T(1024)S(1)} %fusion.44, s32[1280]{0:T(1024)S(1)} %fusion.42, pred[1280]{0:T(1024)(128)(4,1)S(1)} %fusion.49, ...), kind=kOutput, calls=%fused_computation.15 | convolution fusion | flops 2699558912 | bytes 13928448 | tf_op jit(solution)/shard_map/dot_general | solution.py:91
  98.1 2.5 fusion.23
  100.7 0.9 copy.52
  101.7 44.6 %all-gather.5.cloned.1.call-done = bf16[256,4096]{1,0:T(8,128)(2,1)} async-done(((bf16[64,4096]{1,0:T(8,128)(2,1)}), bf16[256,4096]{1,0:T(8,128)(2,1)}) %all-gather.5.cloned.1.call-update) | async-done | bytes 2097168 | tf_op jit(solution)/shard_map/all_gather | solution.py:99
  146.2 10.7 %convolution_convert_fusion.2 = bf16[256,1792]{1,0:T(8,128)(2,1)} fusion(bf16[256,4096]{1,0:T(8,128)(2,1)} %all-gather.5.cloned.1.call-done, bf16[4096,1792]{1,0:T(8,128)(2,1)} %param.27), kind=kOutput, calls=%fused_computation.21 | convolution fusion | flops 3758555136 | bytes 17694720 | tf_op jit(solution)/shard_map/dot_general | solution.py:102
  158.0 21.9 %reduce-scatter.3.cloned.1.call-done = bf16[64,1792]{1,0:T(8,128)(2,1)} async-done(((bf16[256,1792]{1,0:T(8,128)(2,1)}), bf16[64,1792]{1,0:T(8,128)(2,1)}) %reduce-scatter.3.cloned.1.call-update) | async-done | bytes 229392 | tf_op jit(solution)/shard_map/reduce_scatter | solution.py:101
  180.0 1.0 add_convert_fusion
  181.0 21.0 %all_gather.19 = bf16[64,7168]{1,0:T(8,128)(2,1)S(1)} all-gather(bf16[64,1792]{1,0:T(8,128)(2,1)S(1)} %add_convert_fusion), channel_id=1, replica_groups=mesh['groups'=2,'seq'=4,'expert'=4] {'seq'}, dimensions={1}, use_global_device_ids=true | all-gather | bytes 1146880 | tf_op jit(solution)/shard_map/all_gather | solution.py:123
  202.3 0.8 convolution_convert_fusion.1
  203.1 30.6 %all_to_all.10 = bf16[4,40,7168]{2,1,0:T(8,128)(2,1)S(1)} all-to-all(bf16[4,40,7168]{2,1,0:T(8,128)(2,1)S(1)} %bitcast.44), channel_id=1, replica_groups=mesh['groups'=2,'seq'=4,'expert'=4] {'expert'}, dimensions={0} | all-to-all | bytes 4587520 | tf_op jit(solution)/shard_map/all_to_all | solution.py:131
  233.7 0.8 fusion.12
  234.5 1.3 copy-done.11
  235.7 0.8 fusion.32
  236.5 1.3 copy-done.12
  237.8 2.2 convolution_convert_fusion
  240.0 45.3 %reduce-scatter.5.cloned.1.call-done = bf16[4,40,1792]{2,1,0:T(8,128)(2,1)} async-done(((bf16[4,40,7168]{2,1,0:T(8,128)(2,1)}), bf16[4,40,1792]{2,1,0:T(8,128)(2,1)}) %reduce-scatter.5.cloned.1.call-update) | async-done | bytes 573456 | tf_op jit(solution)/shard_map/reduce_scatter | solution.py:20
  285.3 3.5 %all-to-all-start.1 = ((bf16[4,40,1792]{2,1,0:T(8,128)(2,1)}), bf16[4,40,1792]{2,1,0:T(8,128)(2,1)S(1)}, u32[]{:S(2)}, u32[]{:S(2)}) async-start(bf16[4,40,1792]{2,1,0:T(8,128)(2,1)} %reduce-scatter.5.cloned.1.call-done), calls=%async_computation.3 | async-start | bytes 1146880 | tf_op jit(solution)/shard_map/all_to_all | solution.py:23
  288.9 9.2 %all-to-all-done.1 = bf16[4,40,1792]{2,1,0:T(8,128)(2,1)S(1)} async-done(((bf16[4,40,1792]{2,1,0:T(8,128)(2,1)}), bf16[4,40,1792]{2,1,0:T(8,128)(2,1)S(1)}, u32[]{:S(2)}, u32[]{:S(2)}) %all-to-all-start.1) | async-done | bytes 573472 | tf_op jit(solution)/shard_map/all_to_all | solution.py:23
  298.0 1.1 convolution_convert_fusion.3
  (54 shorter events, 1.9 us)
Async XLA Ops:
  7.2 33.7 %copy-start.6 = (bf16[64,512]{1,0:T(8,128)(2,1)S(1)}, bf16[64,512]{1,0:T(8,128)(2,1)}, u32[]{:S(2)}) copy-start(bf16[64,512]{1,0:T(8,128)(2,1)} %param.24) | copy-start | bytes 196612
  7.2 33.7 %copy-start.8 = (bf16[64,64]{1,0:T(8,128)(2,1)S(1)}, bf16[64,64]{1,0:T(8,128)(2,1)}, u32[]{:S(2)}) copy-start(bf16[64,64]{1,0:T(8,128)(2,1)} %param.25) | copy-start | bytes 24580
  7.2 34.6 %copy-start.2 = (bf16[64,16384]{1,0:T(8,128)(2,1)S(1)}, bf16[64,16384]{1,0:T(8,128)(2,1)}, u32[]{:S(2)}) copy-start(bf16[64,16384]{1,0:T(8,128)(2,1)} %param.17) | copy-start | bytes 6291460
  7.2 74.1 %all-gather.3.cloned.1.call-start = ((), (), s32[]{:S(2)}) async-start(), calls=%async_computation.4 | async-start | bytes 2048000 | tf_op jit(solution)/shard_map/all_gather | solution.py:70
  37.9 6.3 %copy-start.4 = (bf16[64,2048]{1,0:T(8,128)(2,1)S(1)}, bf16[64,2048]{1,0:T(8,128)(2,1)}, u32[]{:S(2)}) copy-start(bf16[64,2048]{1,0:T(8,128)(2,1)} %param.18) | copy-start | bytes 786436
  41.7 104.5 %all-gather.5.cloned.1.call-start = ((), (), s32[]{:S(2)}) async-start(), calls=%async_computation.5 | async-start | bytes 2621440 | tf_op jit(solution)/shard_map/all_gather | solution.py:99
  81.3 5.1 %copy-start.7 = (bf16[1280,576]{1,0:T(8,128)(2,1)S(1)}, bf16[1280,576]{1,0:T(8,128)(2,1)}, u32[]{:S(2)}) copy-start(bf16[1280,576]{1,0:T(8,128)(2,1)} %all-gather.3.cloned.1.call-done) | copy-start | bytes 4423684
  93.6 4.5 %copy-start = (bf16[32,512,128]{2,1,0:T(8,128)(2,1)S(1)}, bf16[32,512,128]{2,1,0:T(8,128)(2,1)}, u32[]{:S(2)}) copy-start(bf16[32,512,128]{2,1,0:T(8,128)(2,1)} %param.26) | copy-start | bytes 12582916
  101.6 55.4 %copy-start.9 = (s32[64,2]{0,1:T(2,128)S(1)}, s32[64,2]{0,1:T(2,128)}, u32[]{:S(2)}) copy-start(s32[64,2]{0,1:T(2,128)} %param.29) | copy-start | bytes 1540
  101.6 78.4 %copy-start.5 = (bf16[64,1792]{1,0:T(8,128)(2,1)S(1)}, bf16[64,1792]{1,0:T(8,128)(2,1)}, u32[]{:S(2)}) copy-start(bf16[64,1792]{1,0:T(8,128)(2,1)} %param.28) | copy-start | bytes 688132
  101.6 78.3 %reduce-scatter.3.cloned.1.call-start = ((), (), s32[]{:S(2)}) async-start(), calls=%async_computation.6 | async-start | bytes 1146880 | tf_op jit(solution)/shard_map/reduce_scatter | solution.py:101
  157.0 128.3 %reduce-scatter.5.cloned.1.call-start = ((), (), s32[]{:S(2)}) async-start(), calls=%async_computation.7 | async-start | bytes 2867200 | tf_op jit(solution)/shard_map/reduce_scatter | solution.py:20
  181.0 52.7 %copy-start.3 = (bf16[64,1792]{1,0:T(8,128)(2,1)}, bf16[64,1792]{1,0:T(8,128)(2,1)S(1)}, u32[]{:S(2)}) copy-start(bf16[64,1792]{1,0:T(8,128)(2,1)S(1)} %add_convert_fusion) | copy-start | bytes 688132
  202.3 31.4 %copy-start.1 = (bf16[1,7168,256]{2,1,0:T(8,128)(2,1)S(1)}, bf16[1,7168,256]{2,1,0:T(8,128)(2,1)}, u32[]{:S(2)}) copy-start(bf16[1,7168,256]{2,1,0:T(8,128)(2,1)} %param.31) | copy-start | bytes 11010052
  233.7 2.0 copy-start.11
  235.7 2.0 copy-start.12
  237.8 51.0 %copy-start.10 = (f32[64,2]{0,1:T(2,128)S(1)}, f32[64,2]{0,1:T(2,128)}, u32[]{:S(2)}) copy-start(f32[64,2]{0,1:T(2,128)} %param.30) | copy-start | bytes 1540
  285.3 12.8 %all-to-all-start.1 = ((bf16[4,40,1792]{2,1,0:T(8,128)(2,1)}), bf16[4,40,1792]{2,1,0:T(8,128)(2,1)S(1)}, u32[]{:S(2)}, u32[]{:S(2)}) async-start(bf16[4,40,1792]{2,1,0:T(8,128)(2,1)} %reduce-scatter.5.cloned.1.call-done), calls=%async_computation.3 | async-start | bytes 1146880 | tf_op jit(solution)/shard_map/all_to_all | solution.py:23
Sparse Core Ops, SparseCore 0:
  41.8 39.4 all-gather.2
  101.7 44.4 all-gather.4
  157.1 22.8 reduce-scatter.2
  240.1 45.1 reduce-scatter.4
